TPU v7x, 256 devices: a whole 4x4x8 slice. The times are simulated.
256 devices in a mesh: seq: 32 (over z, y), mp: 8 (over x, core).
Axes of the slice: x: 4, y: 4, z: 8, core: 2. Of those that a mesh axis runs over, the one named last changes fastest.
Arguments:
- tokens: bfloat16 [12288, 4096], P('seq', 'mp'), may hold values from -6 to 6
- norm_gain: float32 [2, 4096], replicated, may hold values from 0.25 to 1.75
- in_weight: bfloat16 [2, 3, 4096, 4096], P(None, None, 'seq', 'mp'), may hold values from -0.09375 to 0.09375
- feat_filter: float32 [2, 3, 3, 4096], P(None, None, None, 'mp'), may hold values from -3 to 3
- short_filter: float32 [256, 7], P('mp'), may hold values from -3 to 3
- medium_filter: float32 [256, 128], P('mp'), may hold values from -0.4 to 0.4
- out_weight: bfloat16 [4096, 4096], P('seq', 'mp'), may hold values from -0.09375 to 0.09375
Outputs:
- stream: bfloat16 [12288, 4096], P('seq', 'mp')
- mixed: bfloat16 [12288, 4096], P('seq', 'mp')
All inputs are finite; a program needn't handle non-finite values.
Results may differ from a plain program's by a relative error of at most 0.015.
Values may be sent and summed in bfloat16 or wider, within the bound.
A program may use at most 128 MiB of HBM per device.

v0:
```python
import jax
import jax.numpy as jnp
from jax import lax
from jax.sharding import PartitionSpec as P


def shifted(x, axis, by):
    peers = lax.axis_size(axis)
    pairs = [(i, i + by) for i in range(peers) if 0 <= i + by < peers]
    return lax.ppermute(x, axis, pairs)


def causal_taps(extended, taps, count):
    reach = taps.shape[0] - 1
    offset = extended.shape[0] - count - reach
    values = extended.astype(jnp.float32)
    total = jnp.zeros((count, extended.shape[1]), jnp.float32)
    for index in range(reach + 1):
        begin = offset + reach - index
        total = total + taps[index] * values[begin : begin + count]
    return total


def toeplitz_conv(kv_ext, filt, count):
    width = filt.shape[1]
    channels = kv_ext.shape[1]
    groups_here = filt.shape[0]
    per_group = channels // groups_here
    padded = jnp.concatenate([jnp.zeros((1, channels), kv_ext.dtype), kv_ext], axis=0)
    blocks = padded.astype(jnp.float32).reshape(count // width + 1, width, groups_here, per_group)
    lag = jnp.arange(width)[:, None] - jnp.arange(width)[None, :]
    current = jnp.where(lag >= 0, filt[:, jnp.clip(lag, 0, width - 1)], 0.0)
    earlier = jnp.where(lag < 0, filt[:, jnp.clip(lag + width, 0, width - 1)], 0.0)
    out = jnp.einsum("gik,bkgc->bigc", current, blocks[1:], precision=lax.Precision.HIGHEST)
    out = out + jnp.einsum("gik,bkgc->bigc", earlier, blocks[:-1], precision=lax.Precision.HIGHEST)
    return out.reshape(count, channels)


def normalized(stream_loc, gain):
    full = lax.all_gather(stream_loc, "mp", axis=1, tiled=True)
    values = full.astype(jnp.float32)
    mean_sq = jnp.mean(values * values, axis=-1, keepdims=True)
    return (values * lax.rsqrt(mean_sq + 1e-06) * gain).astype(jnp.bfloat16)


def project(normed, weights):
    return jnp.einsum(
        "rd,cdf->crf",
        normed,
        lax.all_gather(weights, "seq", axis=1, tiled=True),
        preferred_element_type=jnp.float32,
    ).astype(jnp.bfloat16)


def gated_mix(proj, feat_taps, inner_fn, span):
    rows = proj.shape[1]
    reach = feat_taps.shape[1] - 1
    rim = shifted(proj[:, rows - reach :, :], "seq", 1)
    extended = jnp.concatenate([rim, proj], axis=1)
    query = causal_taps(extended[0], feat_taps[0], rows)
    key_part = causal_taps(extended[1], feat_taps[1], rows)
    value_part = causal_taps(extended[2], feat_taps[2], rows)
    kv_prod = (key_part * value_part).astype(jnp.bfloat16)
    earlier = shifted(kv_prod[rows - span :], "seq", 1)
    kv_ext = jnp.concatenate([earlier, kv_prod], axis=0)
    inner = inner_fn(kv_ext, rows)
    return (query * inner).astype(jnp.bfloat16)


def local(tokens, norm_gain, in_weight, feat_filter, short_filter, medium_filter, out_weight):
    per_group = tokens.shape[1] // short_filter.shape[0]
    short_taps = jnp.repeat(short_filter.T, per_group, axis=1)

    def short_inner(kv_ext, count):
        return causal_taps(kv_ext, short_taps, count)

    def medium_inner(kv_ext, count):
        return toeplitz_conv(kv_ext, medium_filter, count)

    normed = normalized(tokens, norm_gain[0])
    proj = project(normed, in_weight[0])
    first = gated_mix(proj, feat_filter[0], short_inner, short_filter.shape[1] - 1)
    first_full = lax.all_gather(first, "mp", axis=1, tiled=True)
    delta = jnp.dot(
        first_full,
        lax.all_gather(out_weight, "seq", axis=0, tiled=True),
        preferred_element_type=jnp.float32,
    )
    stream = (tokens.astype(jnp.float32) + delta).astype(jnp.bfloat16)
    normed_next = normalized(stream, norm_gain[1])
    proj_next = project(normed_next, in_weight[1])
    mixed = gated_mix(proj_next, feat_filter[1], medium_inner, medium_filter.shape[1] - 1)
    return (stream, mixed)


def solution(mesh):
    placed = (
        P("seq", "mp"),
        P(),
        P(None, None, "seq", "mp"),
        P(None, None, None, "mp"),
        P("mp", None),
        P("mp", None),
        P("seq", "mp"),
    )
    return jax.shard_map(
        local,
        mesh=mesh,
        in_specs=placed,
        out_specs=(P("seq", "mp"), P("seq", "mp")),
        check_vma=False,
    )
```

profile of v0, /device:TPU:88, one launch (start us, length us, event | category | flops | bytes accessed | tf_op | source)
XLA Modules:
  0.0 597.8 jit_solution(11730328731184018714)
XLA Ops:
  7.9 2.1 fusion.119
  10.8 0.9 fusion.121
  11.7 30.4 %all-gather.9.cloned.1.call-done = bf16[384,4096]{1,0:T(8,128)(2,1)} async-done(((bf16[384,512]{1,0:T(8,128)(2,1)}), bf16[384,4096]{1,0:T(8,128)(2,1)}) %all-gather.9.cloned.1.call-update) | async-done | bytes 3145744 | tf_op jit(solution)/shard_map/all_gather | solution.py:40
  42.1 2.7 fusion.4
  44.9 116.5 %all-gather.17.cloned.1.call-done = bf16[1,3,4096,512]{3,2,1,0:T(8,128)(2,1)} async-done(((bf16[1,3,128,512]{3,2,1,0:T(8,128)(2,1)}), bf16[1,3,4096,512]{3,2,1,0:T(8,128)(2,1)}) %all-gather.17.cloned.1.call-update) | async-done | bytes 12582928 | tf_op jit(solution)/shard_map/all_gather | solution.py:50
  161.4 8.3 %fusion.39 = bf16[3,384,512]{2,1,0:T(8,128)(2,1)S(1)} fusion(bf16[1,3,4096,512]{3,2,1,0:T(8,128)(2,1)} %all-gather.17.cloned.1.call-done, bf16[384,4096]{1,0:T(8,128)(2,1)S(1)} %copy-done.1, f32[4096]{0:T(1024)S(1)} %bitcast.255, f32[384]{0:T(512)S(1)} %add_rsqrt_fusion.1), kind=kOutput, calls=%fused_computation.35 | convolution fusion | flops 4838719488 | bytes 16926208 | tf_op jit(solution)/shard_map/rd,cdf->crf/dot_general | solution.py:47
  169.7 6.5 %collective-permute-start = (bf16[3,2,512]{2,1,0:T(2,128)(2,1)S(1)}, bf16[3,2,512]{2,1,0:T(2,128)(2,1)S(1)}, u32[]{:S(2)}, u32[]{:S(2)}) collective-permute-start(bf16[3,2,512]{2,1,0:T(2,128)(2,1)S(1)} %slice.436), channel_id=1, source_target_pairs={{0,8},{8,16},{16,24},{24,32},{32,40},{40,48},{48,56},{56,64},{64,7... | collective-permute-start | bytes 18440 | tf_op jit(solution)/shard_map/ppermute | solution.py:10
  176.8 0.7 collective-permute-done
  178.3 6.3 %collective-permute-start.1 = (bf16[6,512]{1,0:T(8,128)(2,1)S(1)}, bf16[6,512]{1,0:T(8,128)(2,1)S(1)}, u32[]{:S(2)}, u32[]{:S(2)}) collective-permute-start(bf16[6,512]{1,0:T(8,128)(2,1)S(1)} %slice.450), channel_id=1, source_target_pairs={{0,8},{8,16},{16,24},{24,32},{32,40},{40,48},{48,56},{56,64},{64,7... | collective-permute-start | bytes 18440 | tf_op jit(solution)/shard_map/ppermute | solution.py:10
  186.1 1.7 fusion.76
  187.9 55.7 %all-gather.13.cloned.1.call-done = bf16[4096,512]{1,0:T(8,128)(2,1)} async-done(((bf16[128,512]{1,0:T(8,128)(2,1)}), bf16[4096,512]{1,0:T(8,128)(2,1)}) %all-gather.13.cloned.1.call-update) | async-done | bytes 4194320 | tf_op jit(solution)/shard_map/all_gather | solution.py:86
  243.6 32.9 %all-gather.11.cloned.1.call-done = bf16[384,4096]{1,0:T(8,128)(2,1)} async-done(((bf16[384,512]{1,0:T(8,128)(2,1)}), bf16[384,4096]{1,0:T(8,128)(2,1)}) %all-gather.11.cloned.1.call-update) | async-done | bytes 3145744 | tf_op jit(solution)/shard_map/all_gather | solution.py:83
  276.5 5.7 fusion.50
  282.8 29.9 %all-gather.15.cloned.1.call-done = bf16[384,4096]{1,0:T(8,128)(2,1)} async-done(((bf16[384,512]{1,0:T(8,128)(2,1)}), bf16[384,4096]{1,0:T(8,128)(2,1)}) %all-gather.15.cloned.1.call-update) | async-done | bytes 3145744 | tf_op jit(solution)/shard_map/all_gather | solution.py:40
  312.7 2.7 fusion.7
  315.4 116.4 %all-gather.19.cloned.1.call-done = bf16[1,3,4096,512]{3,2,1,0:T(8,128)(2,1)} async-done(((bf16[1,3,128,512]{3,2,1,0:T(8,128)(2,1)}), bf16[1,3,4096,512]{3,2,1,0:T(8,128)(2,1)}) %all-gather.19.cloned.1.call-update) | async-done | bytes 12582928 | tf_op jit(solution)/shard_map/all_gather | solution.py:50
  431.8 8.2 %fusion.34 = bf16[3,384,512]{2,1,0:T(8,128)(2,1)S(1)} fusion(bf16[1,3,4096,512]{3,2,1,0:T(8,128)(2,1)} %all-gather.19.cloned.1.call-done, bf16[384,4096]{1,0:T(8,128)(2,1)S(1)} %copy-done.2, f32[4096]{0:T(1024)S(1)} %bitcast.254, f32[384]{0:T(512)S(1)} %add_rsqrt_fusion), kind=kOutput, calls=%fused_computation.34 | convolution fusion | flops 4838719488 | bytes 16926208 | tf_op jit(solution)/shard_map/rd,cdf->crf/dot_general | solution.py:47
  440.1 6.5 %collective-permute-start.2 = (bf16[3,2,512]{2,1,0:T(2,128)(2,1)S(1)}, bf16[3,2,512]{2,1,0:T(2,128)(2,1)S(1)}, u32[]{:S(2)}, u32[]{:S(2)}) collective-permute-start(bf16[3,2,512]{2,1,0:T(2,128)(2,1)S(1)} %slice.458), channel_id=1, source_target_pairs={{0,8},{8,16},{16,24},{24,32},{32,40},{40,48},{48,56},{56,64},{64,7... | collective-permute-start | bytes 18440 | tf_op jit(solution)/shard_map/ppermute | solution.py:10
  446.7 1.3 collective-permute-done.2
  448.8 6.5 %collective-permute-start.3 = (bf16[127,512]{1,0:T(8,128)(2,1)S(1)}, bf16[127,512]{1,0:T(8,128)(2,1)}, u32[]{:S(2)}, u32[]{:S(2)}) collective-permute-start(bf16[127,512]{1,0:T(8,128)(2,1)S(1)} %slice.472), channel_id=1, source_target_pairs={{0,8},{8,16},{16,24},{24,32},{32,40},{40,48},{48,56},{56,64},{64,7... | collective-permute-start | bytes 390152 | tf_op jit(solution)/shard_map/ppermute | solution.py:10
  456.0 54.8 %gather_fusion.1 = f32[16384,32]{1,0:T(8,128)} fusion(f32[32,128]{0,1:T(8,128)S(1)} %copy.17, s32[16384]{0:T(1024)S(1)} %fusion.114), kind=kCustom, calls=%fused_computation.1 | custom fusion | bytes 4259840 | tf_op jit(solution)/shard_map/gather | solution.py:33
  510.8 5.5 copy.22
  516.3 54.8 %gather_fusion = f32[16384,32]{1,0:T(8,128)} fusion(f32[32,128]{0,1:T(8,128)S(1)} %copy.17, s32[16384]{0:T(1024)S(1)} %fusion.112), kind=kCustom, calls=%fused_computation | custom fusion | bytes 4259840 | tf_op jit(solution)/shard_map/gather | solution.py:32
  571.1 6.4 %copy.18 = f32[128,128,32]{1,0,2:T(8,128)} copy(f32[128,128,32]{2,1,0:T(8,128)} %bitcast.250) | data formatting | bytes 4194304 | tf_op jit(solution)/shard_map/gather | solution.py:32
  577.5 0.9 copy.16
  578.4 2.0 slice.428
  580.5 1.8 pad_maximum_fusion.2
  582.3 1.2 copy.20
  583.5 0.9 slice.431
  584.4 2.9 fusion.18
  587.4 1.8 fusion.47
  590.0 1.0 fusion.70
  (74 shorter events, 7.5 us)
Async XLA Ops:
  7.2 35.0 %all-gather.9.cloned.1.call-start = ((), (), s32[]{:S(2)}) async-start(), calls=%async_computation | async-start | bytes 3538944 | tf_op jit(solution)/shard_map/all_gather | solution.py:40
  7.9 153.5 %all-gather.17.cloned.1.call-start = ((), (), s32[]{:S(2)}) async-start(), calls=%async_computation.4 | async-start | bytes 12976128 | tf_op jit(solution)/shard_map/all_gather | solution.py:50
  10.0 233.5 %all-gather.13.cloned.1.call-start = ((), (), s32[]{:S(2)}) async-start(), calls=%async_computation.2 | async-start | bytes 4325376 | tf_op jit(solution)/shard_map/all_gather | solution.py:86
  10.8 265.7 %all-gather.11.cloned.1.call-start = ((), (), s32[]{:S(2)}) async-start(), calls=%async_computation.1 | async-start | bytes 3538944 | tf_op jit(solution)/shard_map/all_gather | solution.py:83
  42.1 119.3 %copy-start.1 = (bf16[384,4096]{1,0:T(8,128)(2,1)S(1)}, bf16[384,4096]{1,0:T(8,128)(2,1)}, u32[]{:S(2)}) copy-start(bf16[384,4096]{1,0:T(8,128)(2,1)} %all-gather.9.cloned.1.call-done) | copy-start | bytes 9437188
  161.4 14.8 %copy-start.6 = (f32[2,3,3,512]{3,0,2,1:T(2,128)S(1)}, f32[2,3,3,512]{3,0,2,1:T(2,128)}, u32[]{:S(2)}) copy-start(f32[2,3,3,512]{3,0,2,1:T(2,128)} %param.10) | copy-start | bytes 110596
  169.7 7.8 %collective-permute-start = (bf16[3,2,512]{2,1,0:T(2,128)(2,1)S(1)}, bf16[3,2,512]{2,1,0:T(2,128)(2,1)S(1)}, u32[]{:S(2)}, u32[]{:S(2)}) collective-permute-start(bf16[3,2,512]{2,1,0:T(2,128)(2,1)S(1)} %slice.436), channel_id=1, source_target_pairs={{0,8},{8,16},{16,24},{24,32},{32,40},{40,48},{48,56},{56,64},{64,7... | collective-permute-start | bytes 18440 | tf_op jit(solution)/shard_map/ppermute | solution.py:10
  177.8 6.8 %copy-start.11 = (f32[32,7]{0,1:T(8,128)S(1)}, f32[32,7]{0,1:T(8,128)}, u32[]{:S(2)}) copy-start(f32[32,7]{0,1:T(8,128)} %param.11) | copy-start | bytes 2692
  178.3 7.7 %collective-permute-start.1 = (bf16[6,512]{1,0:T(8,128)(2,1)S(1)}, bf16[6,512]{1,0:T(8,128)(2,1)S(1)}, u32[]{:S(2)}, u32[]{:S(2)}) collective-permute-start(bf16[6,512]{1,0:T(8,128)(2,1)S(1)} %slice.450), channel_id=1, source_target_pairs={{0,8},{8,16},{16,24},{24,32},{32,40},{40,48},{48,56},{56,64},{64,7... | collective-permute-start | bytes 18440 | tf_op jit(solution)/shard_map/ppermute | solution.py:10
  186.1 90.3 %copy-start.4 = (bf16[384,512]{1,0:T(8,128)(2,1)S(1)}, bf16[384,512]{1,0:T(8,128)(2,1)}, u32[]{:S(2)}) copy-start(bf16[384,512]{1,0:T(8,128)(2,1)} %param.7) | copy-start | bytes 1179652
  187.8 124.9 %all-gather.15.cloned.1.call-start = ((), (), s32[]{:S(2)}) async-start(), calls=%async_computation.3 | async-start | bytes 3538944 | tf_op jit(solution)/shard_map/all_gather | solution.py:40
  282.2 149.6 %all-gather.19.cloned.1.call-start = ((), (), s32[]{:S(2)}) async-start(), calls=%async_computation.5 | async-start | bytes 12976128 | tf_op jit(solution)/shard_map/all_gather | solution.py:50
  312.7 119.1 %copy-start.2 = (bf16[384,4096]{1,0:T(8,128)(2,1)S(1)}, bf16[384,4096]{1,0:T(8,128)(2,1)}, u32[]{:S(2)}) copy-start(bf16[384,4096]{1,0:T(8,128)(2,1)} %all-gather.15.cloned.1.call-done) | copy-start | bytes 9437188
  440.1 7.8 %collective-permute-start.2 = (bf16[3,2,512]{2,1,0:T(2,128)(2,1)S(1)}, bf16[3,2,512]{2,1,0:T(2,128)(2,1)S(1)}, u32[]{:S(2)}, u32[]{:S(2)}) collective-permute-start(bf16[3,2,512]{2,1,0:T(2,128)(2,1)S(1)} %slice.458), channel_id=1, source_target_pairs={{0,8},{8,16},{16,24},{24,32},{32,40},{40,48},{48,56},{56,64},{64,7... | collective-permute-start | bytes 18440 | tf_op jit(solution)/shard_map/ppermute | solution.py:10
  448.2 7.7 %copy-start.7 = (f32[32,128]{1,0:T(8,128)S(1)}, f32[32,128]{1,0:T(8,128)}, u32[]{:S(2)}) copy-start(f32[32,128]{1,0:T(8,128)} %param.12) | copy-start | bytes 49156
  448.8 131.7 %collective-permute-start.3 = (bf16[127,512]{1,0:T(8,128)(2,1)S(1)}, bf16[127,512]{1,0:T(8,128)(2,1)}, u32[]{:S(2)}, u32[]{:S(2)}) collective-permute-start(bf16[127,512]{1,0:T(8,128)(2,1)S(1)} %slice.472), channel_id=1, source_target_pairs={{0,8},{8,16},{16,24},{24,32},{32,40},{40,48},{48,56},{56,64},{64,7... | collective-permute-start | bytes 390152 | tf_op jit(solution)/shard_map/ppermute | solution.py:10
  577.5 6.9 %copy-start.5 = (pred[128,128]{1,0:T(8,128)(4,1)S(1)}, pred[128,128]{1,0:T(8,128)(4,1)}, u32[]{:S(2)}) copy-start(pred[128,128]{1,0:T(8,128)(4,1)} %fusion.115) | copy-start | bytes 49156
  584.4 3.0 copy-start
  584.4 3.0 copy-start.3
  589.1 0.8 copy-start.8
  589.1 0.8 copy-start.9
  589.1 0.8 copy-start.10
Sparse Core Ops, SparseCore 0:
  9.8 32.2 all-gather.8
  45.3 116.0 all-gather.16
  164.0 79.5 all-gather.12
  245.8 30.5 all-gather.10
  282.3 30.3 all-gather.14
  315.7 116.0 all-gather.18
where the time goes:
time: 598 us
  waiting for transfers between devices  386 us (65%)
  local copies, waits for them, and re-layouts  132 us (22%)
  matrix products  26.9 us (4%)
  starting transfers between devices  26 us (4%)
  between operations  14.4 us (2%)
  other arithmetic  12.3 us (2%)
    all_gather x2, waiting for transfers between devices, project(): lax.all_gather(weights, 'seq', axis=1, tiled=True)  233 us
    gather x2, local copies, waits for them, and re-layouts, toeplitz_conv(): current = jnp.where(lag >= 0, filt[:, jnp.clip(lag, 0, width - 1)], 0.0)  61.2 us
    all_gather x2, waiting for transfers between devices, normalized(): full = lax.all_gather(stream_loc, 'mp', axis=1, tiled=True)  60.3 us
    gather x2, local copies, waits for them, and re-layouts, toeplitz_conv(): filt[:, jnp.clip(lag + width, 0, width - 1)]  60.3 us
    all_gather x1, waiting for transfers between devices, local(): lax.all_gather(out_weight, 'seq', axis=0, tiled=True)  55.7 us
    all_gather x1, waiting for transfers between devices, local(): first_full = lax.all_gather(first, 'mp', axis=1, tiled=True)  32.9 us
    ppermute x4, starting transfers between devices, shifted(): return lax.ppermute(x, axis, pairs)  25.8 us
    dot_general x2, matrix products, project(): jnp.einsum('rd,cdf->crf', normed, lax.all_gather(weights, 'seq', axis=1,...  16.5 us
  transfers between devices with their start and end apart: 10, of which 9 were waited for; matrix products, arithmetic and copies ran while one was open for 24% of the time, Pallas kernels for 0%

commit v1 on v0

--- a/solution.py
+++ b/solution.py
@@ -37,7 +37,16 @@
 
 
 def normalized(stream_loc, gain):
-    full = lax.all_gather(stream_loc, "mp", axis=1, tiled=True)
+    ways = lax.axis_size("mp")
+    up = [(d, (d + 1) % ways) for d in range(ways)]
+    down = [(d, (d - 1) % ways) for d in range(ways)]
+    earlier_2, later = ([stream_loc], [stream_loc])
+    for _ in range(ways // 2):
+        earlier_2.append(lax.ppermute(earlier_2[-1], "mp", up))
+    for _ in range((ways - 1) // 2):
+        later.append(lax.ppermute(later[-1], "mp", down))
+    line = jnp.concatenate([*earlier_2[::-1], *later[1:]], axis=1)
+    full = jnp.roll(line, (lax.axis_index("mp") - ways // 2) * stream_loc.shape[1], axis=1)
     values = full.astype(jnp.float32)
     mean_sq = jnp.mean(values * values, axis=-1, keepdims=True)
     return (values * lax.rsqrt(mean_sq + 1e-06) * gain).astype(jnp.bfloat16)

time: 598 us -> 531 us (0.89)
  waiting for transfers between devices: 386 us -> 291 us
  starting transfers between devices: 26 us -> 44.7 us
  local copies, waits for them, and re-layouts: 132 us -> 140 us
    all_gather x2, waiting for transfers between devices: 233 us -> 154 us  [project(): lax.all_gather(weights, 'seq', axis=1, tiled=True)]
    all_gather x2 -> x0, waiting for transfers between devices: 60.3 us -> none  [normalized(): full = lax.all_gather(stream_loc, 'mp', axis=1, tiled=True)]
    ppermute x0 -> x14, waiting for transfers between devices: none -> 47.6 us  [the longest x8 47.5 us: normalized(): earlier_2.append(lax.ppermute(earlier_2[-1], 'mp', up))]
    ppermute x0 -> x14, starting transfers between devices: none -> 18.5 us  [the longest x6 18.2 us: normalized(): later.append(lax.ppermute(later[-1], 'mp', down))]
    unnamed x26 -> x58, local copies, waits for them, and re-layouts: 0.22 us -> 6.64 us
  transfers between devices with their start and end apart: 10 -> 22, of which waited for: 9 -> 16; matrix products, arithmetic and copies ran while one was open for 24% -> 29% of each run, Pallas kernels for 0% -> 0%
where the time goes in v1:
time: 531 us; the launch traced here: 530 us
  waiting for transfers between devices  291 us (55%)
  local copies, waits for them, and re-layouts  140 us (26%)
  starting transfers between devices  44.7 us (8%)
  matrix products  28.2 us (5%)
  between operations  14.4 us (3%)
  other arithmetic  11.5 us (2%)
    all_gather x2, waiting for transfers between devices, project(): lax.all_gather(weights, 'seq', axis=1, tiled=True)  154 us
    gather x2, local copies, waits for them, and re-layouts, toeplitz_conv(): current = jnp.where(lag >= 0, filt[:, jnp.clip(lag, 0, width - 1)], 0.0)  60.9 us
    gather x2, local copies, waits for them, and re-layouts, toeplitz_conv(): filt[:, jnp.clip(lag + width, 0, width - 1)]  59.9 us
    all_gather x1, waiting for transfers between devices, local(): lax.all_gather(out_weight, 'seq', axis=0, tiled=True)  53.5 us
    ppermute x8, waiting for transfers between devices, normalized(): earlier_2.append(lax.ppermute(earlier_2[-1], 'mp', up))  47.5 us
    all_gather x1, waiting for transfers between devices, local(): first_full = lax.all_gather(first, 'mp', axis=1, tiled=True)  33 us
    ppermute x4, starting transfers between devices, shifted(): return lax.ppermute(x, axis, pairs)  25.8 us
    dot_general x2, matrix products, project(): jnp.einsum('rd,cdf->crf', normed, lax.all_gather(weights, 'seq', axis=1,...  19.8 us
  transfers between devices with their start and end apart: 22, of which 16 were waited for; matrix products, arithmetic and copies ran while one was open for 29% of the time, Pallas kernels for 0%

profile of v1, /device:TPU:88, one launch (start us, length us, event | category | flops | bytes accessed | tf_op | source)
XLA Modules:
  0.0 530.3 jit_solution(18371910110335068892)
XLA Ops:
  7.2 2.1 fusion.123
  10.2 8.6 %collective-permute-done = bf16[384,512]{1,0:T(8,128)(2,1)S(1)} collective-permute-done((bf16[384,512]{1,0:T(8,128)(2,1)}, bf16[384,512]{1,0:T(8,128)(2,1)S(1)}, u32[]{:S(2)}, u32[]{:S(2)}) %collective-permute-start) | collective-permute-done | bytes 393248 | tf_op jit(solution)/shard_map/ppermute | solution.py:45
  19.5 3.0 collective-permute-start.4
  22.5 5.5 %collective-permute-done.1 = bf16[384,512]{1,0:T(8,128)(2,1)S(1)} collective-permute-done((bf16[384,512]{1,0:T(8,128)(2,1)S(1)}, bf16[384,512]{1,0:T(8,128)(2,1)S(1)}, u32[]{:S(2)}, u32[]{:S(2)}) %collective-permute-start.1) | collective-permute-done | bytes 393248 | tf_op jit(solution)/shard_map/ppermute | solution.py:45
  28.1 3.4 collective-permute-start.5
  31.5 4.8 collective-permute-done.2
  37.8 3.0 collective-permute-start.6
  40.8 4.1 collective-permute-done.3
  50.4 2.3 fusion.4
  53.3 75.9 %all-gather.11.cloned.1.call-done = bf16[1,3,4096,512]{3,2,1,0:T(8,128)(2,1)} async-done(((bf16[1,3,128,512]{3,2,1,0:T(8,128)(2,1)}), bf16[1,3,4096,512]{3,2,1,0:T(8,128)(2,1)}) %all-gather.11.cloned.1.call-update) | async-done | bytes 12582928 | tf_op jit(solution)/shard_map/all_gather | solution.py:59
  129.2 9.9 %fusion.41 = bf16[3,384,512]{2,1,0:T(8,128)(2,1)S(1)} fusion(bf16[1,3,4096,512]{3,2,1,0:T(8,128)(2,1)} %all-gather.11.cloned.1.call-done, f32[4096]{0:T(1024)} %bitcast.255, f32[384]{0:T(512)} %add_rsqrt_fusion.1, s32[]{:T(128)S(6)} %select_n.46, bf16[384,4096]{1,0:T(8,128)(2,1)S(1)} %constant_dynamic-update-slice_fusion), kind=kOutput, calls=%fused_computation.41 | convolution fusion | flops 4843438080 | bytes 16926212 | tf_op jit(solution)/shard_map/rd,cdf->crf/dot_general | solution.py:56
  139.1 6.5 %collective-permute-start.7 = (bf16[3,2,512]{2,1,0:T(2,128)(2,1)S(1)}, bf16[3,2,512]{2,1,0:T(2,128)(2,1)S(1)}, u32[]{:S(2)}, u32[]{:S(2)}) collective-permute-start(bf16[3,2,512]{2,1,0:T(2,128)(2,1)S(1)} %slice.436), channel_id=1, source_target_pairs={{0,8},{8,16},{16,24},{24,32},{32,40},{40,48},{48,56},{56,64},{64,7... | collective-permute-start | bytes 18440 | tf_op jit(solution)/shard_map/ppermute | solution.py:10
  147.8 6.3 %collective-permute-start.8 = (bf16[6,512]{1,0:T(8,128)(2,1)S(1)}, bf16[6,512]{1,0:T(8,128)(2,1)S(1)}, u32[]{:S(2)}, u32[]{:S(2)}) collective-permute-start(bf16[6,512]{1,0:T(8,128)(2,1)S(1)} %slice.450), channel_id=1, source_target_pairs={{0,8},{8,16},{16,24},{24,32},{32,40},{40,48},{48,56},{56,64},{64,7... | collective-permute-start | bytes 18440 | tf_op jit(solution)/shard_map/ppermute | solution.py:10
  157.8 53.5 %all-gather.9.cloned.1.call-done = bf16[4096,512]{1,0:T(8,128)(2,1)} async-done(((bf16[128,512]{1,0:T(8,128)(2,1)}), bf16[4096,512]{1,0:T(8,128)(2,1)}) %all-gather.9.cloned.1.call-update) | async-done | bytes 4194320 | tf_op jit(solution)/shard_map/all_gather | solution.py:95
  211.3 33.0 %all-gather.7.cloned.1.call-done = bf16[384,4096]{1,0:T(8,128)(2,1)} async-done(((bf16[384,512]{1,0:T(8,128)(2,1)}), bf16[384,4096]{1,0:T(8,128)(2,1)}) %all-gather.7.cloned.1.call-update) | async-done | bytes 3145744 | tf_op jit(solution)/shard_map/all_gather | solution.py:92
  244.4 4.9 fusion.52
  249.6 8.2 %collective-permute-done.9 = bf16[384,512]{1,0:T(8,128)(2,1)S(1)} collective-permute-done((bf16[384,512]{1,0:T(8,128)(2,1)S(1)}, bf16[384,512]{1,0:T(8,128)(2,1)S(1)}, u32[]{:S(2)}, u32[]{:S(2)}) %collective-permute-start.9) | collective-permute-done | bytes 393248 | tf_op jit(solution)/shard_map/ppermute | solution.py:45
  257.7 3.0 collective-permute-start.13
  260.7 5.5 %collective-permute-done.10 = bf16[384,512]{1,0:T(8,128)(2,1)S(1)} collective-permute-done((bf16[384,512]{1,0:T(8,128)(2,1)S(1)}, bf16[384,512]{1,0:T(8,128)(2,1)S(1)}, u32[]{:S(2)}, u32[]{:S(2)}) %collective-permute-start.10) | collective-permute-done | bytes 393248 | tf_op jit(solution)/shard_map/ppermute | solution.py:45
  266.2 3.0 collective-permute-start.14
  269.1 5.5 %collective-permute-done.11 = bf16[384,512]{1,0:T(8,128)(2,1)S(1)} collective-permute-done((bf16[384,512]{1,0:T(8,128)(2,1)S(1)}, bf16[384,512]{1,0:T(8,128)(2,1)S(1)}, u32[]{:S(2)}, u32[]{:S(2)}) %collective-permute-start.11) | collective-permute-done | bytes 393248 | tf_op jit(solution)/shard_map/ppermute | solution.py:45
  274.6 3.0 collective-permute-start.15
  277.6 5.4 %collective-permute-done.12 = bf16[384,512]{1,0:T(8,128)(2,1)S(1)} collective-permute-done((bf16[384,512]{1,0:T(8,128)(2,1)S(1)}, bf16[384,512]{1,0:T(8,128)(2,1)S(1)}, u32[]{:S(2)}, u32[]{:S(2)}) %collective-permute-start.12) | collective-permute-done | bytes 393248 | tf_op jit(solution)/shard_map/ppermute | solution.py:45
  283.4 2.3 fusion.7
  285.7 77.8 %all-gather.13.cloned.1.call-done = bf16[1,3,4096,512]{3,2,1,0:T(8,128)(2,1)} async-done(((bf16[1,3,128,512]{3,2,1,0:T(8,128)(2,1)}), bf16[1,3,4096,512]{3,2,1,0:T(8,128)(2,1)}) %all-gather.13.cloned.1.call-update) | async-done | bytes 12582928 | tf_op jit(solution)/shard_map/all_gather | solution.py:59
  363.5 9.9 %fusion.36 = bf16[3,384,512]{2,1,0:T(8,128)(2,1)S(1)} fusion(bf16[1,3,4096,512]{3,2,1,0:T(8,128)(2,1)} %all-gather.13.cloned.1.call-done, f32[4096]{0:T(1024)S(1)} %bitcast.254, f32[384]{0:T(512)S(1)} %add_rsqrt_fusion, s32[]{:T(128)S(6)} %select_n.46, bf16[384,4096]{1,0:T(8,128)(2,1)S(1)} %constant_dynamic-update-slice_fusion.8), kind=kOutput, calls=%fused_computation.40 | convolution fusion | flops 4843438080 | bytes 16926212 | tf_op jit(solution)/shard_map/rd,cdf->crf/dot_general | solution.py:56
  373.5 6.5 %collective-permute-start.16 = (bf16[3,2,512]{2,1,0:T(2,128)(2,1)S(1)}, bf16[3,2,512]{2,1,0:T(2,128)(2,1)S(1)}, u32[]{:S(2)}, u32[]{:S(2)}) collective-permute-start(bf16[3,2,512]{2,1,0:T(2,128)(2,1)S(1)} %slice.458), channel_id=1, source_target_pairs={{0,8},{8,16},{16,24},{24,32},{32,40},{40,48},{48,56},{56,64},{64,7... | collective-permute-start | bytes 18440 | tf_op jit(solution)/shard_map/ppermute | solution.py:10
  382.8 6.5 %collective-permute-start.17 = (bf16[127,512]{1,0:T(8,128)(2,1)}, bf16[127,512]{1,0:T(8,128)(2,1)}, u32[]{:S(2)}, u32[]{:S(2)}) collective-permute-start(bf16[127,512]{1,0:T(8,128)(2,1)} %slice.472), channel_id=1, source_target_pairs={{0,8},{8,16},{16,24},{24,32},{32,40},{40,48},{48,56},{56,64},{64,7... | collective-permute-start | bytes 390152 | tf_op jit(solution)/shard_map/ppermute | solution.py:10
  389.5 54.4 %gather_fusion.1 = f32[16384,32]{1,0:T(8,128)} fusion(f32[32,128]{0,1:T(8,128)S(1)} %copy.17, s32[16384]{0:T(1024)S(1)} %fusion.116), kind=kCustom, calls=%fused_computation.1 | custom fusion | bytes 4259840 | tf_op jit(solution)/shard_map/gather | solution.py:33
  443.9 5.5 %copy.22 = f32[128,128,32]{1,0,2:T(8,128)S(1)} copy(f32[128,128,32]{2,1,0:T(8,128)} %bitcast.251) | data formatting | bytes 4194304 | tf_op jit(solution)/shard_map/gather | solution.py:33
  449.4 54.4 %gather_fusion = f32[16384,32]{1,0:T(8,128)} fusion(f32[32,128]{0,1:T(8,128)S(1)} %copy.17, s32[16384]{0:T(1024)S(1)} %fusion.114), kind=kCustom, calls=%fused_computation | custom fusion | bytes 4259840 | tf_op jit(solution)/shard_map/gather | solution.py:32
  503.8 6.4 %copy.18 = f32[128,128,32]{1,0,2:T(8,128)} copy(f32[128,128,32]{2,1,0:T(8,128)} %bitcast.250) | data formatting | bytes 4194304 | tf_op jit(solution)/shard_map/gather | solution.py:32
  (130 shorter events, 32.0 us)
Async XLA Ops:
  7.2 42.0 %copy-start.2 = (bf16[384,512]{1,0:T(8,128)(2,1)S(1)}, bf16[384,512]{1,0:T(8,128)(2,1)}, u32[]{:S(2)}) copy-start(bf16[384,512]{1,0:T(8,128)(2,1)} %param.9) | copy-start | bytes 1179652
  7.2 122.0 %all-gather.11.cloned.1.call-start = ((), (), s32[]{:S(2)}) async-start(), calls=%async_computation.2 | async-start | bytes 12976128 | tf_op jit(solution)/shard_map/all_gather | solution.py:59
  9.4 202.0 %all-gather.9.cloned.1.call-start = ((), (), s32[]{:S(2)}) async-start(), calls=%async_computation.1 | async-start | bytes 4325376 | tf_op jit(solution)/shard_map/all_gather | solution.py:95
  10.1 234.3 %all-gather.7.cloned.1.call-start = ((), (), s32[]{:S(2)}) async-start(), calls=%async_computation | async-start | bytes 3538944 | tf_op jit(solution)/shard_map/all_gather | solution.py:92
  10.2 8.6 %collective-permute-start = (bf16[384,512]{1,0:T(8,128)(2,1)}, bf16[384,512]{1,0:T(8,128)(2,1)S(1)}, u32[]{:S(2)}, u32[]{:S(2)}) collective-permute-start(bf16[384,512]{1,0:T(8,128)(2,1)} %param.9), channel_id=1, source_target_pairs={{0,1},{1,2},{2,3},{3,4},{4,5},{5,6},{6,7},{7,0},{8,9},{9,10},{10,1... | collective-permute-start | bytes 1179656 | tf_op jit(solution)/shard_map/ppermute | solution.py:45
  19.5 8.4 %collective-permute-start.1 = (bf16[384,512]{1,0:T(8,128)(2,1)S(1)}, bf16[384,512]{1,0:T(8,128)(2,1)S(1)}, u32[]{:S(2)}, u32[]{:S(2)}) collective-permute-start(bf16[384,512]{1,0:T(8,128)(2,1)S(1)} %collective-permute-done), channel_id=1, source_target_pairs={{0,1},{1,2},{2,3},{3,4},{4,5},{5,6},{6,7},{7,0},{8,9},{9,10},{10,1... | collective-permute-start | bytes 1179656 | tf_op jit(solution)/shard_map/ppermute | solution.py:45
  19.5 8.6 %collective-permute-start.4 = (bf16[384,512]{1,0:T(8,128)(2,1)}, bf16[384,512]{1,0:T(8,128)(2,1)S(1)}, u32[]{:S(2)}, u32[]{:S(2)}) collective-permute-start(bf16[384,512]{1,0:T(8,128)(2,1)} %param.9), channel_id=1, source_target_pairs={{0,7},{1,0},{2,1},{3,2},{4,3},{5,4},{6,5},{7,6},{8,15},{9,8},{10,9... | collective-permute-start | bytes 1179656 | tf_op jit(solution)/shard_map/ppermute | solution.py:47
  28.0 12.8 %copy-start.7 = (bf16[384,512]{1,0:T(8,128)(2,1)}, bf16[384,512]{1,0:T(8,128)(2,1)S(1)}, u32[]{:S(2)}) copy-start(bf16[384,512]{1,0:T(8,128)(2,1)S(1)} %collective-permute-done.1) | copy-start | bytes 1179652
  28.0 8.4 %collective-permute-start.2 = (bf16[384,512]{1,0:T(8,128)(2,1)S(1)}, bf16[384,512]{1,0:T(8,128)(2,1)S(1)}, u32[]{:S(2)}, u32[]{:S(2)}) collective-permute-start(bf16[384,512]{1,0:T(8,128)(2,1)S(1)} %collective-permute-done.1), channel_id=1, source_target_pairs={{0,1},{1,2},{2,3},{3,4},{4,5},{5,6},{6,7},{7,0},{8,9},{9,10},{10,1... | collective-permute-start | bytes 1179656 | tf_op jit(solution)/shard_map/ppermute | solution.py:45
  28.1 12.7 %copy-start.5 = (bf16[384,512]{1,0:T(8,128)(2,1)}, bf16[384,512]{1,0:T(8,128)(2,1)S(1)}, u32[]{:S(2)}) copy-start(bf16[384,512]{1,0:T(8,128)(2,1)S(1)} %collective-permute-done.4) | copy-start | bytes 1179652
  28.1 9.7 %collective-permute-start.5 = (bf16[384,512]{1,0:T(8,128)(2,1)S(1)}, bf16[384,512]{1,0:T(8,128)(2,1)}, u32[]{:S(2)}, u32[]{:S(2)}) collective-permute-start(bf16[384,512]{1,0:T(8,128)(2,1)S(1)} %collective-permute-done.4), channel_id=1, source_target_pairs={{0,7},{1,0},{2,1},{3,2},{4,3},{5,4},{6,5},{7,6},{8,15},{9,8},{10,9... | collective-permute-start | bytes 1179656 | tf_op jit(solution)/shard_map/ppermute | solution.py:47
  36.4 8.5 %collective-permute-start.3 = (bf16[384,512]{1,0:T(8,128)(2,1)S(1)}, bf16[384,512]{1,0:T(8,128)(2,1)}, u32[]{:S(2)}, u32[]{:S(2)}) collective-permute-start(bf16[384,512]{1,0:T(8,128)(2,1)S(1)} %collective-permute-done.2), channel_id=1, source_target_pairs={{0,1},{1,2},{2,3},{3,4},{4,5},{5,6},{6,7},{7,0},{8,9},{9,10},{10,1... | collective-permute-start | bytes 1179656 | tf_op jit(solution)/shard_map/ppermute | solution.py:45
  37.8 12.5 %collective-permute-start.6 = (bf16[384,512]{1,0:T(8,128)(2,1)}, bf16[384,512]{1,0:T(8,128)(2,1)S(1)}, u32[]{:S(2)}, u32[]{:S(2)}) collective-permute-start(bf16[384,512]{1,0:T(8,128)(2,1)} %collective-permute-done.5), channel_id=1, source_target_pairs={{0,7},{1,0},{2,1},{3,2},{4,3},{5,4},{6,5},{7,6},{8,15},{9,8},{10,9... | collective-permute-start | bytes 1179656 | tf_op jit(solution)/shard_map/ppermute | solution.py:47
  129.2 16.5 %copy-start.9 = (f32[2,3,3,512]{3,0,2,1:T(2,128)S(1)}, f32[2,3,3,512]{3,0,2,1:T(2,128)}, u32[]{:S(2)}) copy-start(f32[2,3,3,512]{3,0,2,1:T(2,128)} %param.12) | copy-start | bytes 110596
  139.1 7.8 %collective-permute-start.7 = (bf16[3,2,512]{2,1,0:T(2,128)(2,1)S(1)}, bf16[3,2,512]{2,1,0:T(2,128)(2,1)S(1)}, u32[]{:S(2)}, u32[]{:S(2)}) collective-permute-start(bf16[3,2,512]{2,1,0:T(2,128)(2,1)S(1)} %slice.436), channel_id=1, source_target_pairs={{0,8},{8,16},{16,24},{24,32},{32,40},{40,48},{48,56},{56,64},{64,7... | collective-permute-start | bytes 18440 | tf_op jit(solution)/shard_map/ppermute | solution.py:10
  147.8 7.7 %collective-permute-start.8 = (bf16[6,512]{1,0:T(8,128)(2,1)S(1)}, bf16[6,512]{1,0:T(8,128)(2,1)S(1)}, u32[]{:S(2)}, u32[]{:S(2)}) collective-permute-start(bf16[6,512]{1,0:T(8,128)(2,1)S(1)} %slice.450), channel_id=1, source_target_pairs={{0,8},{8,16},{16,24},{24,32},{32,40},{40,48},{48,56},{56,64},{64,7... | collective-permute-start | bytes 18440 | tf_op jit(solution)/shard_map/ppermute | solution.py:10
  157.3 206.2 %all-gather.13.cloned.1.call-start = ((), (), s32[]{:S(2)}) async-start(), calls=%async_computation.3 | async-start | bytes 12976128 | tf_op jit(solution)/shard_map/all_gather | solution.py:59
  249.3 34.0 %copy-start.3 = (bf16[384,512]{1,0:T(8,128)(2,1)}, bf16[384,512]{1,0:T(8,128)(2,1)S(1)}, u32[]{:S(2)}) copy-start(bf16[384,512]{1,0:T(8,128)(2,1)S(1)} %fusion.52) | copy-start | bytes 1179652
  249.3 8.4 %collective-permute-start.9 = (bf16[384,512]{1,0:T(8,128)(2,1)S(1)}, bf16[384,512]{1,0:T(8,128)(2,1)S(1)}, u32[]{:S(2)}, u32[]{:S(2)}) collective-permute-start(bf16[384,512]{1,0:T(8,128)(2,1)S(1)} %fusion.52), channel_id=1, source_target_pairs={{0,1},{1,2},{2,3},{3,4},{4,5},{5,6},{6,7},{7,0},{8,9},{9,10},{10,1... | collective-permute-start | bytes 1179656 | tf_op jit(solution)/shard_map/ppermute | solution.py:45
  257.7 8.4 %collective-permute-start.10 = (bf16[384,512]{1,0:T(8,128)(2,1)S(1)}, bf16[384,512]{1,0:T(8,128)(2,1)S(1)}, u32[]{:S(2)}, u32[]{:S(2)}) collective-permute-start(bf16[384,512]{1,0:T(8,128)(2,1)S(1)} %collective-permute-done.9), channel_id=1, source_target_pairs={{0,1},{1,2},{2,3},{3,4},{4,5},{5,6},{6,7},{7,0},{8,9},{9,10},{10,1... | collective-permute-start | bytes 1179656 | tf_op jit(solution)/shard_map/ppermute | solution.py:45
  257.7 8.4 %collective-permute-start.13 = (bf16[384,512]{1,0:T(8,128)(2,1)S(1)}, bf16[384,512]{1,0:T(8,128)(2,1)S(1)}, u32[]{:S(2)}, u32[]{:S(2)}) collective-permute-start(bf16[384,512]{1,0:T(8,128)(2,1)S(1)} %fusion.52), channel_id=1, source_target_pairs={{0,7},{1,0},{2,1},{3,2},{4,3},{5,4},{6,5},{7,6},{8,15},{9,8},{10,9... | collective-permute-start | bytes 1179656 | tf_op jit(solution)/shard_map/ppermute | solution.py:47
  266.2 8.4 %collective-permute-start.11 = (bf16[384,512]{1,0:T(8,128)(2,1)S(1)}, bf16[384,512]{1,0:T(8,128)(2,1)S(1)}, u32[]{:S(2)}, u32[]{:S(2)}) collective-permute-start(bf16[384,512]{1,0:T(8,128)(2,1)S(1)} %collective-permute-done.10), channel_id=1, source_target_pairs={{0,1},{1,2},{2,3},{3,4},{4,5},{5,6},{6,7},{7,0},{8,9},{9,10},{10,1... | collective-permute-start | bytes 1179656 | tf_op jit(solution)/shard_map/ppermute | solution.py:45
  266.2 8.4 %collective-permute-start.14 = (bf16[384,512]{1,0:T(8,128)(2,1)S(1)}, bf16[384,512]{1,0:T(8,128)(2,1)S(1)}, u32[]{:S(2)}, u32[]{:S(2)}) collective-permute-start(bf16[384,512]{1,0:T(8,128)(2,1)S(1)} %collective-permute-done.13), channel_id=1, source_target_pairs={{0,7},{1,0},{2,1},{3,2},{4,3},{5,4},{6,5},{7,6},{8,15},{9,8},{10,9... | collective-permute-start | bytes 1179656 | tf_op jit(solution)/shard_map/ppermute | solution.py:47
  274.6 8.4 %collective-permute-start.12 = (bf16[384,512]{1,0:T(8,128)(2,1)S(1)}, bf16[384,512]{1,0:T(8,128)(2,1)S(1)}, u32[]{:S(2)}, u32[]{:S(2)}) collective-permute-start(bf16[384,512]{1,0:T(8,128)(2,1)S(1)} %collective-permute-done.11), channel_id=1, source_target_pairs={{0,1},{1,2},{2,3},{3,4},{4,5},{5,6},{6,7},{7,0},{8,9},{9,10},{10,1... | collective-permute-start | bytes 1179656 | tf_op jit(solution)/shard_map/ppermute | solution.py:45
  274.6 8.7 %collective-permute-start.15 = (bf16[384,512]{1,0:T(8,128)(2,1)S(1)}, bf16[384,512]{1,0:T(8,128)(2,1)S(1)}, u32[]{:S(2)}, u32[]{:S(2)}) collective-permute-start(bf16[384,512]{1,0:T(8,128)(2,1)S(1)} %collective-permute-done.14), channel_id=1, source_target_pairs={{0,7},{1,0},{2,1},{3,2},{4,3},{5,4},{6,5},{7,6},{8,15},{9,8},{10,9... | collective-permute-start | bytes 1179656 | tf_op jit(solution)/shard_map/ppermute | solution.py:47
  373.4 8.2 %copy-start.14 = (f32[1,1,1,512]{3,0,2,1:T(1,128)S(1)}, f32[1,1,1,512]{3,0,2,1:T(1,128)}, u32[]{:S(2)}) copy-start(f32[1,1,1,512]{3,0,2,1:T(1,128)} %get-tuple-element.12) | copy-start | bytes 6148
  373.4 8.2 %copy-start.15 = (f32[1,1,1,512]{3,0,2,1:T(1,128)S(1)}, f32[1,1,1,512]{3,0,2,1:T(1,128)}, u32[]{:S(2)}) copy-start(f32[1,1,1,512]{3,0,2,1:T(1,128)} %get-tuple-element.13) | copy-start | bytes 6148
  373.4 8.2 %copy-start.16 = (f32[1,1,1,512]{3,0,2,1:T(1,128)S(1)}, f32[1,1,1,512]{3,0,2,1:T(1,128)}, u32[]{:S(2)}) copy-start(f32[1,1,1,512]{3,0,2,1:T(1,128)} %get-tuple-element.14) | copy-start | bytes 6148
  373.4 8.2 %copy-start.17 = (f32[1,1,1,512]{3,0,2,1:T(1,128)S(1)}, f32[1,1,1,512]{3,0,2,1:T(1,128)}, u32[]{:S(2)}) copy-start(f32[1,1,1,512]{3,0,2,1:T(1,128)} %get-tuple-element.15) | copy-start | bytes 6148
  373.4 8.2 %copy-start.18 = (f32[1,1,1,512]{3,0,2,1:T(1,128)S(1)}, f32[1,1,1,512]{3,0,2,1:T(1,128)}, u32[]{:S(2)}) copy-start(f32[1,1,1,512]{3,0,2,1:T(1,128)} %get-tuple-element.27) | copy-start | bytes 6148
  373.5 7.8 %collective-permute-start.16 = (bf16[3,2,512]{2,1,0:T(2,128)(2,1)S(1)}, bf16[3,2,512]{2,1,0:T(2,128)(2,1)S(1)}, u32[]{:S(2)}, u32[]{:S(2)}) collective-permute-start(bf16[3,2,512]{2,1,0:T(2,128)(2,1)S(1)} %slice.458), channel_id=1, source_target_pairs={{0,8},{8,16},{16,24},{24,32},{32,40},{40,48},{48,56},{56,64},{64,7... | collective-permute-start | bytes 18440 | tf_op jit(solution)/shard_map/ppermute | solution.py:10
  382.8 130.4 %collective-permute-start.17 = (bf16[127,512]{1,0:T(8,128)(2,1)}, bf16[127,512]{1,0:T(8,128)(2,1)}, u32[]{:S(2)}, u32[]{:S(2)}) collective-permute-start(bf16[127,512]{1,0:T(8,128)(2,1)} %slice.472), channel_id=1, source_target_pairs={{0,8},{8,16},{16,24},{24,32},{32,40},{40,48},{48,56},{56,64},{64,7... | collective-permute-start | bytes 390152 | tf_op jit(solution)/shard_map/ppermute | solution.py:10
  (11 other events, 38.3 us)
Sparse Core Ops, SparseCore 0:
  11.2 117.9 all-gather.10
  131.8 79.5 all-gather.8
  213.8 30.5 all-gather.6
  247.4 116.0 all-gather.12
